TPU v7x, 512 devices: a whole 4x8x8 slice. The times are simulated.
512 devices in a mesh: row: 64 (over y_hi, x, z), col: 8 (over y_lo, core).
Axes of the slice: x: 4, y: 8 (y_hi: 2, y_lo: 4; y = y_hi * 4 + y_lo), z: 8, core: 2. Of those that a mesh axis runs over, the one named last changes fastest.
Arguments:
- features: bfloat16 [131072, 256], P(('row', 'col')), may hold values from -6 to 6
- weight: bfloat16 [256, 256], replicated, may hold values from -0.375 to 0.375
- weight_self: bfloat16 [256, 256], replicated, may hold values from -0.375 to 0.375
- tile_values: bfloat16 [64, 256, 128, 128], P('row', 'col'), may hold values from -0.125 to 0.125
- tile_rows: int32 [64, 256], P('row', 'col'), may hold values from 0 to 1
- tile_cols: int32 [64, 256], P('row', 'col'), may hold values from 0 to 47
- tile_count: int32 [64, 8], P('row', 'col'), may hold values from 1 to 32, as said below
- cotangent: bfloat16 [131072, 256], P(('row', 'col')), may hold values from -6 to 6
Outputs:
- activations: bfloat16 [131072, 256], P(('row', 'col'))
- feature_grad: bfloat16 [131072, 256], P(('row', 'col'))
- weight_grad: float32 [256, 256], replicated
- self_grad: float32 [256, 256], replicated
Inputs may be any that keep to these rules, and one draw needn't show every extreme that they name: Slots 0 to tile_count - 1 of a node block are live, the others are ignored; some node block has all 32 slots live.
All inputs are finite; a program needn't handle non-finite values.
Results may differ from a plain program's by a relative error of at most 0.0052.
Values may be sent and summed in bfloat16 or wider, within the bound.
A program may use at most 64 MiB of HBM per device.

v0:
```python
import math
import jax
import jax.numpy as jnp
from jax import lax
from jax.sharding import PartitionSpec as P


def with_halo(cells, sides, width):
    for axis, dim in sides:
        count = lax.axis_size(axis)
        head = lax.slice_in_dim(cells, 0, width, axis=dim)
        tail = lax.slice_in_dim(cells, cells.shape[dim] - width, cells.shape[dim], axis=dim)
        cells = jnp.concatenate(
            [
                lax.ppermute(tail, axis, [(i, (i + 1) % count) for i in range(count)]),
                cells,
                lax.ppermute(head, axis, [((i + 1) % count, i) for i in range(count)]),
            ],
            axis=dim,
        )
    return cells


def passed_along(value, axis, steps):
    count = lax.axis_size(axis)
    pairs = [(source, (source + steps) % count) for source in range(count)]
    return lax.ppermute(value, axis, pairs)


def shards(features, weight, weight_self, tile_values, tile_rows, tile_cols, tile_count, cotangent):
    tile_block = tile_values[0]
    slot_rows = tile_rows[0]
    slot_cols = tile_cols[0]
    live_count = tile_count[0, 0]
    slot_total = tile_block.shape[0]
    tile_side = tile_block.shape[-1]
    node_rows = features.shape[0]
    width = features.shape[1]
    per_block = node_rows // tile_side
    col_count = lax.axis_size("col")
    row_count = lax.axis_size("row")
    span = col_count * per_block
    group = lax.all_gather(features, "col", axis=0, tiled=True)
    window = with_halo(group, (("row", 0),), group.shape[0])
    window_tiles = window.reshape(-1, tile_side, width)
    row_ids = jnp.arange(per_block, dtype=jnp.int32)
    tiles_part = tile_block
    rows_part = slot_rows
    live_part = jnp.arange(slot_total, dtype=jnp.int32) < live_count
    feat_tiles = window_tiles[slot_cols]
    selector = ((rows_part[None, :] == row_ids[:, None]) & live_part[None, :]).astype(jnp.bfloat16)
    masked = tiles_part[None, :, :, :] * selector[:, :, None, None]
    summed = jnp.einsum("ktij,tjf->kif", masked, feat_tiles, preferred_element_type=jnp.float32)
    aggregated = summed.reshape(node_rows, width).astype(jnp.bfloat16)
    pre_act = jnp.dot(aggregated, weight, preferred_element_type=jnp.float32) + jnp.dot(
        features, weight_self, preferred_element_type=jnp.float32
    )
    activations = jax.nn.silu(pre_act).astype(jnp.bfloat16)
    sigma = jax.nn.sigmoid(pre_act)
    grad_pre = (cotangent.astype(jnp.float32) * sigma * (1.0 + pre_act * (1.0 - sigma))).astype(
        jnp.bfloat16
    )
    weight_part = jnp.einsum("nf,ng->fg", aggregated, grad_pre, preferred_element_type=jnp.float32)
    self_part = jnp.einsum("nf,ng->fg", features, grad_pre, preferred_element_type=jnp.float32)
    grad_aggregated = jnp.einsum(
        "ng,fg->nf", grad_pre, weight, preferred_element_type=jnp.float32
    ).astype(jnp.bfloat16)
    self_feature = jnp.einsum(
        "ng,fg->nf", grad_pre, weight_self, preferred_element_type=jnp.float32
    )
    grad_tiles = grad_aggregated.reshape(per_block, tile_side, width)
    spread_zero = jnp.zeros((3 * span, tile_side, width), jnp.float32)
    tiles_part = tile_block
    rows_part = slot_rows
    live_part = (jnp.arange(slot_total, dtype=jnp.int32) < live_count).astype(jnp.float32)
    picked = grad_tiles[rows_part]
    products = jnp.einsum("tij,tif->tjf", tiles_part, picked, preferred_element_type=jnp.float32)
    spread = spread_zero.at[slot_cols].add(products * live_part[:, None, None])
    spread = spread.reshape(3, col_count * node_rows, width)
    middle = spread[1]
    for offset in (1, -1):
        outgoing = spread[2] if offset == 1 else spread[0]
        middle = middle + passed_along(outgoing, "row", offset)
    own_share = lax.psum_scatter(middle, "col", scatter_dimension=0, tiled=True)
    feature_grad = (own_share + self_feature).astype(jnp.bfloat16)
    weight_total, self_total = lax.psum((weight_part, self_part), ("row", "col"))
    factor = 1.0 / math.sqrt(node_rows * col_count * row_count)
    return (activations, feature_grad, weight_total * factor, self_total * factor)


def solution(mesh):
    placed = (
        P(("row", "col"), None),
        P(),
        P(),
        P("row", "col", None, None),
        P("row", "col"),
        P("row", "col"),
        P("row", "col"),
        P(("row", "col"), None),
    )
    return jax.shard_map(
        shards,
        mesh=mesh,
        in_specs=placed,
        out_specs=(P(("row", "col"), None), P(("row", "col"), None), P(), P()),
        check_vma=False,
    )
```

profile of v0, /device:TPU:4, one launch (start us, length us, event | category | flops | bytes accessed | tf_op | source)
XLA Modules:
  0.0 519.9 jit_solution(5023080746673470452)
XLA Ops:
  7.2 0.0 copy-start
  7.2 0.0 all-gather.2.cloned.1.call-start
  7.2 0.7 all-gather.2.cloned.1.call-update
  7.9 0.0 all-reduce.3.cloned.1.call-start
  8.6 46.0 %all-gather.2.cloned.1.call-done = bf16[2048,256]{1,0:T(8,128)(2,1)} async-done(((bf16[256,256]{1,0:T(8,128)(2,1)}), bf16[2048,256]{1,0:T(8,128)(2,1)}) %all-gather.2.cloned.1.call-update) | async-done | bytes 1048592 | tf_op jit(solution)/shard_map/all_gather | solution.py:43
  54.6 5.8 %collective-permute-start.1 = (bf16[2048,256]{1,0:T(8,128)(2,1)}, bf16[2048,256]{1,0:T(8,128)(2,1)S(1)}, u32[]{:S(2)}, u32[]{:S(2)}) collective-permute-start(bf16[2048,256]{1,0:T(8,128)(2,1)} %all-gather.2.cloned.1.call-done), channel_id=1, source_target_pairs={{8,0},{16,8},{24,16},{32,24},{40,32},{48,40},{56,48},{64,56},{72,6... | collective-permute-start | bytes 3145736 | tf_op jit(solution)/shard_map/ppermute | solution.py:17
  60.5 1.9 collective-permute-start
  62.4 0.7 fusion.16
  63.1 0.7 fusion.17
  63.8 0.7 and_convert_fusion
  64.4 15.8 %collective-permute-done.1 = bf16[2048,256]{1,0:T(8,128)(2,1)S(1)} collective-permute-done((bf16[2048,256]{1,0:T(8,128)(2,1)}, bf16[2048,256]{1,0:T(8,128)(2,1)S(1)}, u32[]{:S(2)}, u32[]{:S(2)}) %collective-permute-start.1) | collective-permute-done | bytes 1048608 | tf_op jit(solution)/shard_map/ppermute | solution.py:17
  80.3 6.1 %collective-permute-done = bf16[2048,256]{1,0:T(8,128)(2,1)S(1)} collective-permute-done((bf16[2048,256]{1,0:T(8,128)(2,1)}, bf16[2048,256]{1,0:T(8,128)(2,1)S(1)}, u32[]{:S(2)}, u32[]{:S(2)}) %collective-permute-start) | collective-permute-done | bytes 1048608 | tf_op jit(solution)/shard_map/ppermute | solution.py:15
  86.4 1.6 pad_maximum_fusion
  88.0 2.0 gather_fusion
  90.1 2.7 fusion.9
  92.8 0.0 copy-start.5
  92.8 0.0 copy-done.2
  92.8 0.2 fusion.21
  93.0 0.0 copy-done
  93.0 0.0 copy-done.3
  93.0 0.0 copy-done.7
  93.0 0.9 multiply_convert_fusion
  94.0 0.2 convolution_convert_fusion
  94.2 0.0 copy-done.5
  94.2 0.0 copy-start.1
  94.2 0.7 gather_fusion.1
  94.9 0.5 copy-done.1
  95.4 2.9 multiply_bitcast_fusion
  98.3 5.6 %copy.15 = f32[32,128,256]{2,1,0:T(8,128)} copy(f32[32,128,256]{1,2,0:T(8,128)} %multiply_bitcast_fusion) | data formatting | bytes 8388608 | tf_op jit(solution)/shard_map/mul | solution.py:78
  103.9 3.4 broadcast_in_dim.2
  107.3 9.9 %scatter_fusion = f32[48,128,256]{2,1,0:T(8,128)} fusion(f32[48,128,256]{2,1,0:T(8,128)} %broadcast_in_dim.2, s32[32]{0:T(128)S(1)} %fusion.16, f32[32,128,256]{2,1,0:T(8,128)} %copy.15), kind=kCustom, calls=%fused_computation.2 | custom fusion | flops 1048576 | bytes 12583040 | tf_op jit(solution)/shard_map/scatter-add | solution.py:78
  117.3 5.6 %fusion.20 = (f32[16,128,256]{2,1,0:T(8,128)S(1)}, f32[16,128,256]{2,1,0:T(8,128)}, f32[16,128,256]{2,1,0:T(8,128)}) fusion(f32[48,128,256]{2,1,0:T(8,128)} %scatter_fusion), kind=kLoop, calls=%fused_computation.33 | loop fusion | bytes 12582912 | tf_op jit(solution)/shard_map/slice | solution.py:80
  122.9 1.9 collective-permute-start.3
  124.8 3.9 collective-permute-start.2
  128.7 0.0 copy-done.6
  128.7 0.9 fusion.23
  129.7 0.9 convolution_bitcast_fusion
  130.6 0.0 all-reduce.3.cloned.1.call-update
  130.6 0.0 reduce-scatter.2.cloned.1.call-start
  130.7 37.7 %collective-permute-done.3 = f32[2048,256]{1,0:T(8,128)} collective-permute-done((f32[2048,256]{1,0:T(8,128)}, f32[2048,256]{1,0:T(8,128)}, u32[]{:S(2)}, u32[]{:S(2)}) %collective-permute-start.3) | collective-permute-done | bytes 2097184 | tf_op jit(solution)/shard_map/ppermute | solution.py:27
  168.4 4.0 collective-permute-done.2
  172.4 4.0 fusion
  176.4 0.0 reduce-scatter.2.cloned.1.call-update
  176.4 0.2 fusion.22
  176.6 290.9 %all-reduce.3.cloned.1.call-done = (f32[256,256]{1,0:T(8,128)}, f32[256,256]{1,0:T(8,128)}) async-done(((f32[256,256]{1,0:T(8,128)}, f32[256,256]{1,0:T(8,128)}), (f32[256,256]{1,0:T(8,128)}, f32[256,256]{1,0:T(8,128)})) %all-reduce.3.cloned.1.call-update) | async-done | bytes 524304 | tf_op jit(solution)/shard_map/psum | solution.py:86
  467.5 1.9 broadcast_multiply_fusion
  469.4 42.4 %reduce-scatter.2.cloned.1.call-done = f32[256,256]{1,0:T(8,128)} async-done(((f32[2048,256]{1,0:T(8,128)}), f32[256,256]{1,0:T(8,128)}) %reduce-scatter.2.cloned.1.call-update) | async-done | bytes 262160 | tf_op jit(solution)/shard_map/reduce_scatter | solution.py:84
  511.8 1.6 add_convert_fusion
  (10 shorter events, 0.0 us)
Async XLA Ops:
  7.2 85.8 %copy-start = (bf16[256,256]{1,0:T(8,128)(2,1)S(1)}, bf16[256,256]{1,0:T(8,128)(2,1)}, u32[]{:S(2)}) copy-start(bf16[256,256]{1,0:T(8,128)(2,1)} %param.10) | copy-start | bytes 393220
  7.2 47.5 %all-gather.2.cloned.1.call-start = ((), (), s32[]{:S(2)}) async-start(), calls=%async_computation.1 | async-start | bytes 1179648 | tf_op jit(solution)/shard_map/all_gather | solution.py:43
  7.9 459.6 %all-reduce.3.cloned.1.call-start = ((), (), s32[]{:S(2)}) async-start(), calls=%async_computation.3 | async-start | bytes 1048576 | tf_op jit(solution)/shard_map/psum | solution.py:86
  54.6 25.6 %collective-permute-start.1 = (bf16[2048,256]{1,0:T(8,128)(2,1)}, bf16[2048,256]{1,0:T(8,128)(2,1)S(1)}, u32[]{:S(2)}, u32[]{:S(2)}) collective-permute-start(bf16[2048,256]{1,0:T(8,128)(2,1)} %all-gather.2.cloned.1.call-done), channel_id=1, source_target_pairs={{8,0},{16,8},{24,16},{32,24},{40,32},{48,40},{56,48},{64,56},{72,6... | collective-permute-start | bytes 3145736 | tf_op jit(solution)/shard_map/ppermute | solution.py:17
  60.5 25.9 %collective-permute-start = (bf16[2048,256]{1,0:T(8,128)(2,1)}, bf16[2048,256]{1,0:T(8,128)(2,1)S(1)}, u32[]{:S(2)}, u32[]{:S(2)}) collective-permute-start(bf16[2048,256]{1,0:T(8,128)(2,1)} %all-gather.2.cloned.1.call-done), channel_id=1, source_target_pairs={{0,8},{8,16},{16,24},{24,32},{32,40},{40,48},{48,56},{56,64},{64,7... | collective-permute-start | bytes 3145736 | tf_op jit(solution)/shard_map/ppermute | solution.py:15
  90.1 2.7 copy-start.2
  90.1 2.9 copy-start.3
  90.1 2.9 copy-start.7
  92.8 1.4 copy-start.5
  94.2 1.2 copy-start.1
  117.3 11.4 %copy-start.6 = (bf16[2,128,256]{2,1,0:T(8,128)(2,1)S(1)}, bf16[2,128,256]{2,1,0:T(8,128)(2,1)}, u32[]{:S(2)}) copy-start(bf16[2,128,256]{2,1,0:T(8,128)(2,1)} %copy-done.5) | copy-start | bytes 393220
  117.3 12.4 %copy-start.4 = (bf16[256,256]{1,0:T(8,128)(2,1)S(1)}, bf16[256,256]{1,0:T(8,128)(2,1)}, u32[]{:S(2)}) copy-start(bf16[256,256]{1,0:T(8,128)(2,1)} %param.8) | copy-start | bytes 393220
  122.9 45.5 %collective-permute-start.3 = (f32[2048,256]{1,0:T(8,128)}, f32[2048,256]{1,0:T(8,128)}, u32[]{:S(2)}, u32[]{:S(2)}) collective-permute-start(f32[2048,256]{1,0:T(8,128)} %bitcast.16), channel_id=1, source_target_pairs={{0,504},{8,0},{16,8},{24,16},{32,24},{40,32},{48,40},{56,48},{64,5... | collective-permute-start | bytes 6291464 | tf_op jit(solution)/shard_map/ppermute | solution.py:27
  124.8 47.6 %collective-permute-start.2 = (f32[2048,256]{1,0:T(8,128)}, f32[2048,256]{1,0:T(8,128)}, u32[]{:S(2)}, u32[]{:S(2)}) collective-permute-start(f32[2048,256]{1,0:T(8,128)} %bitcast.15), channel_id=1, source_target_pairs={{0,8},{8,16},{16,24},{24,32},{32,40},{40,48},{48,56},{56,64},{64,7... | collective-permute-start | bytes 6291464 | tf_op jit(solution)/shard_map/ppermute | solution.py:27
  130.6 381.2 %reduce-scatter.2.cloned.1.call-start = ((), (), s32[]{:S(2)}) async-start(), calls=%async_computation.2 | async-start | bytes 2359296 | tf_op jit(solution)/shard_map/reduce_scatter | solution.py:84
Sparse Core Ops, SparseCore 0:
  10.1 44.5 all-gather.1
  130.7 336.7 all-reduce.2
  470.6 41.1 reduce-scatter.1
where the time goes:
time: 520 us
  waiting for transfers between devices  444 us (85%)
  other arithmetic  21 us (4%)
  local copies, waits for them, and re-layouts  17.9 us (3%)
  between operations  14.6 us (3%)
  starting transfers between devices  13.7 us (3%)
  matrix products  9.04 us (2%)
    psum x1, waiting for transfers between devices, shards(): lax.psum((weight_part, self_part), ('row', 'col'))  291 us
    all_gather x1, waiting for transfers between devices, shards(): group = lax.all_gather(features, 'col', axis=0, tiled=True)  46 us
    reduce_scatter x1, waiting for transfers between devices, shards(): own_share = lax.psum_scatter(middle, 'col', scatter_dimension=0, tiled=True)  42.4 us
    ppermute x2, waiting for transfers between devices, passed_along(): return lax.ppermute(value, axis, pairs)  41.7 us
    ppermute x1, waiting for transfers between devices, with_halo(): lax.ppermute(head, axis, [((i + 1) % count, i) for i in range(count)])  15.8 us
  transfers between devices with their start and end apart: 7, of which 7 were waited for; matrix products, arithmetic and copies ran while one was open for 2% of the time, Pallas kernels for 0%

commit v1 on v0

--- a/solution.py
+++ b/solution.py
@@ -1,8 +1,16 @@
+import functools
 import math
 import jax
 import jax.numpy as jnp
 from jax import lax
 from jax.sharding import PartitionSpec as P
+
+
+def waves_mix(original, axis_name, row_axis):
+    return lax.psum(lax.psum(original, axis_name), row_axis)
+
+
+hold_slices_on = functools.partial(waves_mix, axis_name="col", row_axis="row")
 
 
 def with_halo(cells, sides, width):
@@ -83,7 +91,7 @@
         middle = middle + passed_along(outgoing, "row", offset)
     own_share = lax.psum_scatter(middle, "col", scatter_dimension=0, tiled=True)
     feature_grad = (own_share + self_feature).astype(jnp.bfloat16)
-    weight_total, self_total = lax.psum((weight_part, self_part), ("row", "col"))
+    weight_total, self_total = hold_slices_on((weight_part, self_part))
     factor = 1.0 / math.sqrt(node_rows * col_count * row_count)
     return (activations, feature_grad, weight_total * factor, self_total * factor)
 

time: 520 us -> 1170 us (2.25)
  the two profiles are of different devices: /device:TPU:4 before, /device:TPU:2 now
where the time goes in v1:
time: 1170 us
  waiting for transfers between devices  1090 us (93%)
  other arithmetic  21.1 us (2%)
  local copies, waits for them, and re-layouts  17.9 us (2%)
  between operations  14.6 us (1%)
  starting transfers between devices  13.8 us (1%)
    psum x2, waiting for transfers between devices, waves_mix(): return lax.psum(lax.psum(original, axis_name), row_axis)  961 us
    reduce_scatter x1, waiting for transfers between devices, shards(): own_share = lax.psum_scatter(middle, 'col', scatter_dimension=0, tiled=True)  63.2 us
    all_gather x1, waiting for transfers between devices, shards(): group = lax.all_gather(features, 'col', axis=0, tiled=True)  46.1 us
  transfers between devices with their start and end apart: 8, of which 6 were waited for; matrix products, arithmetic and copies ran while one was open for 1% of the time, Pallas kernels for 0%

profile of v1, /device:TPU:2, one launch (start us, length us, event | category | flops | bytes accessed | tf_op | source)
XLA Modules:
  0.0 1168.9 jit_solution(9385190563962858838)
XLA Ops:
  7.2 0.0 copy-start
  7.2 0.0 all-gather.2.cloned.1.call-start
  7.2 0.7 all-gather.2.cloned.1.call-update
  7.9 0.0 all-reduce.7.cloned.1.call-start
  8.6 46.1 %all-gather.2.cloned.1.call-done = bf16[2048,256]{1,0:T(8,128)(2,1)} async-done(((bf16[256,256]{1,0:T(8,128)(2,1)}), bf16[2048,256]{1,0:T(8,128)(2,1)}) %all-gather.2.cloned.1.call-update) | async-done | bytes 1048592 | tf_op jit(solution)/shard_map/all_gather | solution.py:51
  54.7 5.8 collective-permute-start.1
  60.5 1.9 collective-permute-start
  62.5 0.7 fusion.16
  63.1 0.7 fusion.17
  63.8 0.7 and_convert_fusion
  64.5 15.8 %collective-permute-done.1 = bf16[2048,256]{1,0:T(8,128)(2,1)S(1)} collective-permute-done((bf16[2048,256]{1,0:T(8,128)(2,1)}, bf16[2048,256]{1,0:T(8,128)(2,1)S(1)}, u32[]{:S(2)}, u32[]{:S(2)}) %collective-permute-start.1) | collective-permute-done | bytes 1048608 | tf_op jit(solution)/shard_map/ppermute | solution.py:25
  80.3 6.1 collective-permute-done
  86.4 1.6 pad_maximum_fusion
  88.0 2.0 gather_fusion
  90.1 2.7 fusion.9
  92.8 0.0 copy-start.5
  92.8 0.2 fusion.21
  93.0 0.9 multiply_convert_fusion
  94.0 0.2 convolution_convert_fusion
  94.2 0.0 copy-done.5
  94.2 0.0 copy-start.1
  94.2 0.7 gather_fusion.1
  94.9 0.5 copy-done.1
  95.4 2.9 multiply_bitcast_fusion
  98.3 5.6 copy.15
  103.9 3.4 broadcast_in_dim.2
  107.4 10.1 scatter_fusion
  117.4 5.6 fusion.20
  123.0 1.9 collective-permute-start.3
  124.9 3.9 collective-permute-start.2
  128.9 0.0 copy-done.6
  128.9 0.9 fusion.23
  129.8 0.0 copy-done.4
  129.8 0.9 convolution_bitcast_fusion
  130.7 0.0 all-reduce.7.cloned.1.call-update
  130.8 0.0 all-reduce.5.cloned.1.call-start
  130.8 144.8 %all-reduce.7.cloned.1.call-done = (f32[256,256]{1,0:T(8,128)}, f32[256,256]{1,0:T(8,128)}) async-done(((f32[256,256]{1,0:T(8,128)}, f32[256,256]{1,0:T(8,128)}), (f32[256,256]{1,0:T(8,128)}, f32[256,256]{1,0:T(8,128)})) %all-reduce.7.cloned.1.call-update) | async-done | bytes 524304 | tf_op jit(solution)/shard_map/psum | solution.py:10
  275.6 0.0 all-reduce.5.cloned.1.call-update
  275.6 0.0 reduce-scatter.2.cloned.1.call-start
  275.7 0.0 collective-permute-done.3
  275.7 0.0 collective-permute-done.2
  275.7 4.0 fusion
  279.6 0.0 reduce-scatter.2.cloned.1.call-update
  279.7 0.2 fusion.22
  279.9 815.8 %all-reduce.5.cloned.1.call-done = (f32[256,256]{1,0:T(8,128)}, f32[256,256]{1,0:T(8,128)}) async-done(((f32[256,256]{1,0:T(8,128)}, f32[256,256]{1,0:T(8,128)}), (f32[256,256]{1,0:T(8,128)}, f32[256,256]{1,0:T(8,128)})) %all-reduce.5.cloned.1.call-update) | async-done | bytes 524304 | tf_op jit(solution)/shard_map/psum | solution.py:10
  1095.7 1.9 broadcast_multiply_fusion
  1097.6 63.2 %reduce-scatter.2.cloned.1.call-done = f32[256,256]{1,0:T(8,128)} async-done(((f32[2048,256]{1,0:T(8,128)}), f32[256,256]{1,0:T(8,128)}) %reduce-scatter.2.cloned.1.call-update) | async-done | bytes 262160 | tf_op jit(solution)/shard_map/reduce_scatter | solution.py:92
  1160.7 1.6 add_convert_fusion
  (13 shorter events, 0.0 us)
Async XLA Ops:
  7.2 85.8 %copy-start = (bf16[256,256]{1,0:T(8,128)(2,1)S(1)}, bf16[256,256]{1,0:T(8,128)(2,1)}, u32[]{:S(2)}) copy-start(bf16[256,256]{1,0:T(8,128)(2,1)} %param.10) | copy-start | bytes 393220
  7.2 47.5 %all-gather.2.cloned.1.call-start = ((), (), s32[]{:S(2)}) async-start(), calls=%async_computation.1 | async-start | bytes 1179648 | tf_op jit(solution)/shard_map/all_gather | solution.py:51
  7.9 267.7 %all-reduce.7.cloned.1.call-start = ((), (), s32[]{:S(2)}) async-start(), calls=%async_computation.4 | async-start | bytes 1048576 | tf_op jit(solution)/shard_map/psum | solution.py:10
  54.7 25.6 %collective-permute-start.1 = (bf16[2048,256]{1,0:T(8,128)(2,1)}, bf16[2048,256]{1,0:T(8,128)(2,1)S(1)}, u32[]{:S(2)}, u32[]{:S(2)}) collective-permute-start(bf16[2048,256]{1,0:T(8,128)(2,1)} %all-gather.2.cloned.1.call-done), channel_id=1, source_target_pairs={{8,0},{16,8},{24,16},{32,24},{40,32},{48,40},{56,48},{64,56},{72,6... | collective-permute-start | bytes 3145736 | tf_op jit(solution)/shard_map/ppermute | solution.py:25
  60.5 25.9 %collective-permute-start = (bf16[2048,256]{1,0:T(8,128)(2,1)}, bf16[2048,256]{1,0:T(8,128)(2,1)S(1)}, u32[]{:S(2)}, u32[]{:S(2)}) collective-permute-start(bf16[2048,256]{1,0:T(8,128)(2,1)} %all-gather.2.cloned.1.call-done), channel_id=1, source_target_pairs={{0,8},{8,16},{16,24},{24,32},{32,40},{40,48},{48,56},{56,64},{64,7... | collective-permute-start | bytes 3145736 | tf_op jit(solution)/shard_map/ppermute | solution.py:23
  90.1 2.7 copy-start.2
  90.1 2.9 copy-start.3
  90.1 2.9 copy-start.7
  92.8 1.4 copy-start.5
  94.2 1.2 copy-start.1
  117.4 11.4 copy-start.6
  117.4 12.4 %copy-start.4 = (bf16[256,256]{1,0:T(8,128)(2,1)S(1)}, bf16[256,256]{1,0:T(8,128)(2,1)}, u32[]{:S(2)}) copy-start(bf16[256,256]{1,0:T(8,128)(2,1)} %param.8) | copy-start | bytes 393220
  123.0 152.6 %collective-permute-start.3 = (f32[2048,256]{1,0:T(8,128)}, f32[2048,256]{1,0:T(8,128)}, u32[]{:S(2)}, u32[]{:S(2)}) collective-permute-start(f32[2048,256]{1,0:T(8,128)} %bitcast.16), channel_id=1, source_target_pairs={{0,504},{8,0},{16,8},{24,16},{32,24},{40,32},{48,40},{56,48},{64,5... | collective-permute-start | bytes 6291464 | tf_op jit(solution)/shard_map/ppermute | solution.py:35
  124.9 150.7 %collective-permute-start.2 = (f32[2048,256]{1,0:T(8,128)}, f32[2048,256]{1,0:T(8,128)}, u32[]{:S(2)}, u32[]{:S(2)}) collective-permute-start(f32[2048,256]{1,0:T(8,128)} %bitcast.15), channel_id=1, source_target_pairs={{0,8},{8,16},{16,24},{24,32},{32,40},{40,48},{48,56},{56,64},{64,7... | collective-permute-start | bytes 6291464 | tf_op jit(solution)/shard_map/ppermute | solution.py:35
  130.8 964.9 %all-reduce.5.cloned.1.call-start = ((), (), s32[]{:S(2)}) async-start(), calls=%async_computation.3 | async-start | bytes 1048576 | tf_op jit(solution)/shard_map/psum | solution.py:10
  275.6 885.1 %reduce-scatter.2.cloned.1.call-start = ((), (), s32[]{:S(2)}) async-start(), calls=%async_computation.2 | async-start | bytes 2359296 | tf_op jit(solution)/shard_map/reduce_scatter | solution.py:92
Sparse Core Ops, SparseCore 0:
  10.1 44.5 all-gather.1
  130.9 144.6 all-reduce.6
  278.8 816.8 all-reduce.4
  1098.4 62.2 reduce-scatter.1
